TPU v7x, 32 devices: a whole 2x2x4 slice. The times are simulated.
32 devices in a mesh: sky: 8 (over z, y), band: 4 (over x, core).
Axes of the slice: x: 2, y: 2, z: 4, core: 2. Of those that a mesh axis runs over, the one named last changes fastest.
Arguments:
- exposures: bfloat16 [8, 4, 1024, 1024], P('sky', 'band'), may hold values from -6 to 6
- inv_variance: bfloat16 [8, 4, 1024, 1024], P('sky', 'band'), may hold values from 0.25 to 4
- mask_planes: int32 [8, 4, 2, 35], P('sky', 'band'), may hold values from 0 to 1073741823, as said below
- sky_columns: int32 [8, 4, 8], replicated, may hold values from 0 to 7, as said below
- basis_rows: float32 [9, 25], replicated, may hold values from -1 to 1
- basis_cols: float32 [9, 25], replicated, may hold values from -1 to 1
- match_coeffs: float32 [8, 4, 9], P('sky', 'band'), may hold values from -2 to 2
- detect_taps: float32 [4, 31], P('band'), may hold values from 0.05 to 0.3
Outputs:
- difference: bfloat16 [8, 4, 1024, 1024], P('sky', 'band')
- detection: float32 [1024, 1024], P('band', 'sky')
Inputs may be any that keep to these rules, and one draw needn't show every extreme that they name: Each row sky_columns[e, b] holds 8 consecutive sky tile columns in order, counted modulo 8; every sky tile column is covered by some exposure of every band. Bit j of mask_planes[e, b, 0, w] marks pixel column 30 w + j of that exposure as bad and bit j of mask_planes[e, b, 1, w] pixel row 30 w + j; bits past 1024 are ignored. In every draw some word has all 30 bits set.
All inputs are finite; a program needn't handle non-finite values.
Results may differ from a plain program's by a relative error of at most 0.0095.
Values may be sent and summed in bfloat16 or wider, within the bound.
No kernel may reach another device: no remote copies, remote signals or barrier semaphores. Data moves between devices by JAX's collectives and lax.ppermute only.
A program may use at most 128 MiB of HBM per device.

v0:
```python
import jax
import jax.numpy as jnp
from jax import lax
from jax.sharding import PartitionSpec as P

TILE = 128
NB = 9
TAPS = 25
DTAPS = 31


def with_halo(block, sides, width):
    for axis, dim in sides:
        count = lax.axis_size(axis)
        forward = [(i, i + 1) for i in range(count - 1)]
        forward.append((count - 1, 0))
        backward = [(target, source) for source, target in forward]
        low = lax.ppermute(
            lax.slice_in_dim(block, block.shape[dim] - width, None, axis=dim), axis, forward
        )
        high = lax.ppermute(lax.slice_in_dim(block, 0, width, axis=dim), axis, backward)
        block = jnp.concatenate([low, block, high], axis=dim)
    return block


def band_matrix(tap_rows, window_width):
    offsets = (
        jnp.arange(window_width, dtype=jnp.int32)[:, None]
        - jnp.arange(TILE, dtype=jnp.int32)[None, :]
    )
    selector = (
        offsets[:, :, None] == jnp.arange(tap_rows.shape[1], dtype=jnp.int32)[None, None, :]
    ).astype(jnp.float32)
    return jnp.einsum(
        "wtl,kl->kwt", selector, tap_rows.astype(jnp.float32), precision=lax.Precision.HIGHEST
    ).astype(jnp.bfloat16)


def keep_pixels(planes, side_length):
    places = jnp.arange(side_length, dtype=jnp.int32)
    column_bits = jnp.bitwise_and(jnp.right_shift(planes[0][places // 30], places % 30), 1)
    row_bits = jnp.bitwise_and(jnp.right_shift(planes[1][places // 30], places % 30), 1)
    return jnp.logical_and(row_bits[:, None] == 0, column_bits[None, :] == 0)


def psf_match(picture, column_taps, row_taps):
    side_length = picture.shape[1]
    block_count = side_length // TILE
    margin = TAPS // 2
    width_full = TILE + 2 * margin
    padded = jnp.pad(picture, ((0, 0), (margin, margin)))
    blocks = jnp.stack(
        [
            padded[:, TILE * block_index : TILE * block_index + width_full]
            for block_index in range(block_count)
        ],
        0,
    )
    column_band = band_matrix(column_taps, width_full)
    column_pass = jnp.einsum(
        "jyw,kwt->kyjt", blocks, column_band, preferred_element_type=jnp.float32
    )
    column_pass = column_pass.reshape(NB, side_length, side_length).astype(jnp.bfloat16)
    row_padded = jnp.pad(column_pass, ((0, 0), (margin, margin), (0, 0)))
    row_blocks = jnp.stack(
        [
            row_padded[:, TILE * block_index : TILE * block_index + width_full, :]
            for block_index in range(block_count)
        ],
        0,
    )
    row_band = band_matrix(row_taps, width_full)
    summed = jnp.einsum("ikwx,kwt->itx", row_blocks, row_band, preferred_element_type=jnp.float32)
    return summed.reshape(side_length, side_length).astype(jnp.bfloat16)


def average_pieces(pieces):
    matched_in, weight_in = pieces
    weight_float = weight_in.astype(jnp.float32)
    numer = jnp.sum(weight_float * matched_in.astype(jnp.float32), axis=1)
    denom = jnp.sum(weight_float, axis=1)
    return (numer / jnp.maximum(denom, 1.0)).astype(jnp.bfloat16)


def subtract_template(template, matched, own_columns, side_length, sky_count):
    gathered = lax.all_gather(template, "sky", axis=1, tiled=True).reshape(
        side_length, sky_count, TILE
    )
    picked = jnp.take(gathered, own_columns, axis=1).reshape(side_length, side_length)
    return (matched.astype(jnp.float32) - picked.astype(jnp.float32)).astype(jnp.bfloat16)


def body(
    exposures,
    inv_variance,
    mask_planes,
    sky_columns,
    basis_rows,
    basis_cols,
    match_coeffs,
    detect_taps,
):
    picture = exposures[0, 0]
    side_length = picture.shape[0]
    block_count = side_length // TILE
    sky_count = lax.axis_size("sky")
    own_sky = lax.axis_index("sky")
    own_band = lax.axis_index("band")
    column_taps = (match_coeffs[0, 0][:, None] * basis_cols).astype(jnp.bfloat16)
    matched = psf_match(picture, column_taps, basis_rows.astype(jnp.bfloat16))
    keep = keep_pixels(mask_planes[0, 0], side_length)
    variance_inv = inv_variance[0, 0]
    weight = jnp.where(keep, variance_inv, jnp.zeros_like(variance_inv))
    own_columns = sky_columns[own_sky, own_band]
    empty_slots = jnp.zeros((side_length, sky_count, TILE), jnp.bfloat16)
    send_matched = empty_slots.at[:, own_columns, :].set(
        matched.reshape(side_length, block_count, TILE)
    )
    send_weight = empty_slots.at[:, own_columns, :].set(
        weight.reshape(side_length, block_count, TILE)
    )
    template = average_pieces(
        (
            lax.all_to_all(send_matched, "sky", split_axis=1, concat_axis=1, tiled=True),
            lax.all_to_all(send_weight, "sky", split_axis=1, concat_axis=1, tiled=True),
        )
    )
    difference = subtract_template(template, matched, own_columns, side_length, sky_count)
    margin = DTAPS // 2
    width_full = TILE + 2 * margin
    filter_band = band_matrix(detect_taps.astype(jnp.bfloat16), width_full)[0]
    widened = with_halo(template, (("sky", 1),), margin)
    smoothed = jnp.dot(widened, filter_band, preferred_element_type=jnp.float32).astype(
        jnp.bfloat16
    )
    smooth_padded = jnp.pad(smoothed, ((margin, margin), (0, 0)))
    smooth_blocks = jnp.stack(
        [
            smooth_padded[TILE * block_index : TILE * block_index + width_full]
            for block_index in range(block_count)
        ],
        0,
    )
    filtered = jnp.einsum(
        "iwx,wt->itx", smooth_blocks, filter_band, preferred_element_type=jnp.float32
    ).reshape(side_length, TILE)
    power = filtered * filtered
    detection = lax.psum_scatter(power, "band", scatter_dimension=0, tiled=True)
    return (difference[None, None], detection)


def solution(mesh):
    in_specs = (
        P("sky", "band", None, None),
        P("sky", "band", None, None),
        P("sky", "band", None, None),
        P(),
        P(),
        P(),
        P("sky", "band", None),
        P("band", None),
    )
    out_specs = (P("sky", "band", None, None), P("band", "sky"))
    return jax.shard_map(body, mesh=mesh, in_specs=in_specs, out_specs=out_specs, check_vma=False)
```

profile of v0, /device:TPU:0, one launch (start us, length us, event | category | flops | bytes accessed | tf_op | source)
XLA Modules:
  0.0 304.6 jit_solution(1016820240146248366)
XLA Ops:
  12.4 9.2 %convolution_convert_fusion = bf16[9,128,8,1024]{3,1,2,0:T(8,128)(2,1)} fusion(bf16[8,1024,152]{1,2,0:T(8,128)(2,1)S(1)} %fusion.34, bf16[9,152,128,1]{2,0,1,3:T(8,128)(2,1)S(1)} %fusion.19), kind=kOutput, calls=%fused_computation.5 | convolution fusion | flops 2878341120 | bytes 21714944 | tf_op jit(solution)/shard_map/jyw,kwt->kyjt/dot_general | solution.py:60
  21.6 24.6 %copy.67 = bf16[9,1024,1024]{2,1,0:T(8,128)(2,1)} copy(bf16[9,1024,1024]{1,2,0:T(8,128)(2,1)} %bitcast.237) | data formatting | bytes 37748736 | tf_op jit(solution)/shard_map/convert_element_type | solution.py:63
  46.3 4.3 %fusion.2 = bf16[8,9,152,1024]{3,2,1,0:T(8,128)(2,1)} fusion(bf16[9,1024,1024]{2,1,0:T(8,128)(2,1)} %copy.67), kind=kLoop, calls=%fused_computation.13 | loop fusion | bytes 21676032
  50.6 3.8 %copy-done = bf16[9,1024,1024]{2,1,0:T(8,128)(2,1)S(1)} copy-done((bf16[9,1024,1024]{2,1,0:T(8,128)(2,1)S(1)}, bf16[9,1024,1024]{2,1,0:T(8,128)(2,1)}, u32[]{:S(2)}) %copy-start) | copy-done | bytes 18874392
  72.2 9.9 %bitcast_convert_fusion = bf16[128,8,1024]{2,0,1:T(8,128)(2,1)S(1)} fusion(bf16[8,9,152,1024]{3,2,1,0:T(8,128)(2,1)} %fusion.4, bf16[9,152,128]{2,0,1:T(8,128)(2,1)S(1)} %fusion.20), kind=kOutput, calls=%fused_computation.9 | convolution fusion | flops 2869952512 | bytes 24860672 | tf_op jit(solution)/shard_map/ikwx,kwt->itx/dot_general | solution.py:73
  86.7 5.7 %scatter_fusion.1 = bf16[1024,8,128]{2,0,1:T(8,128)(2,1)} fusion(bf16[1024,8,128]{2,0,1:T(8,128)(2,1)} %broadcast_in_dim.16.clone.1, s32[8]{0:T(128)S(1)} %fusion.61, bf16[8,1024,128]{2,1,0:T(8,128)(2,1)} %bitcast.248), kind=kCustom, calls=%fused_computation.2 | custom fusion | bytes 6291488 | tf_op jit(solution)/shard_map/scatter | solution.py:116
  92.4 7.3 %all-to-all-start.1 = ((bf16[1024,8,128]{2,0,1:T(8,128)(2,1)}), bf16[1024,8,128]{2,0,1:T(8,128)(2,1)}, u32[]{:S(2)}, u32[]{:S(2)}) async-start(bf16[1024,8,128]{2,0,1:T(8,128)(2,1)} %scatter_fusion.1), calls=%async_computation.1 | async-start | bytes 4194304 | tf_op jit(solution)/shard_map/all_to_all | solution.py:124
  99.8 3.9 %copy.75 = bf16[1,1,1024,1024]{2,3,1,0:T(8,128)(2,1)} copy(bf16[1,1,1024,1024]{3,2,1,0:T(8,128)(2,1)} %param.9) | data formatting | bytes 4194304 | tf_op args[1]
  103.7 3.9 %copy.76 = bf16[1024,8,128]{2,0,1:T(8,128)(2,1)} copy(bf16[1024,8,128]{0,2,1:T(8,128)(2,1)} %bitcast.253) | data formatting | bytes 4194304 | tf_op jit(solution)/shard_map/squeeze | solution.py:112
  110.2 4.6 %compare_select_fusion.2 = s32[1024,1]{0,1:T(1,128)S(1)} fusion(s32[]{:T(128)} %bitcast.99, s32[]{:T(128)} %bitcast.100, s32[]{:T(128)} %bitcast.101, s32[]{:T(128)} %bitcast.102, s32[]{:T(128)} %bitcast.103, s32[]{:T(128)} %bitcast.105, s32[]{:T(128)} %bitcast.104), kind=kLoop, calls=%fused_computation.125 | loop fusion | flops 23552 | bytes 4124 | tf_op jit(solution)/shard_map/gather | solution.py:41
  116.3 4.4 %compare_select_fusion.1 = s32[1024,1]{0,1:T(1,128)S(1)} fusion(s32[]{:T(128)} %bitcast.63, s32[]{:T(128)} %bitcast.64, s32[]{:T(128)} %bitcast.65, s32[]{:T(128)} %bitcast.66, s32[]{:T(128)} %bitcast.67, s32[]{:T(128)} %bitcast.69, s32[]{:T(128)} %bitcast.68), kind=kLoop, calls=%fused_computation.124 | loop fusion | flops 23552 | bytes 4124 | tf_op jit(solution)/shard_map/gather | solution.py:42
  120.6 17.6 %fusion.49 = pred[8,128]{1,0:T(8,128)(4,1)S(1)} fusion(pred[1024]{0:T(1024)(128)(4,1)S(1)} %compare_reduce_fusion, pred[1024]{0:T(1024)(128)(4,1)S(1)} %compare_reduce_fusion.1, pred[1024]{0:T(1024)(128)(4,1)S(1)} %compare_reduce_fusion.2, pred[1024]{0:T(1024)(128)(4,1)S(1)} %compare_reduce_fusion.3, pred[1024]{0:T(1024)(128)(4,1)S(1)} %compare_reduce_fusion.4, ...), kind=kLoop, calls=%fused_computation.147 | loop fusion | flops 39936 | bytes 33904 | tf_op jit(solution)/shard_map/eq | solution.py:43
  138.3 17.6 %fusion.46 = pred[1024]{0:T(1024)(128)(4,1)S(1)} fusion(pred[1024]{0:T(1024)(128)(4,1)S(1)} %compare_reduce_fusion, pred[1024]{0:T(1024)(128)(4,1)S(1)} %compare_reduce_fusion.1, pred[1024]{0:T(1024)(128)(4,1)S(1)} %compare_reduce_fusion.2, pred[1024]{0:T(1024)(128)(4,1)S(1)} %compare_reduce_fusion.3, pred[1024]{0:T(1024)(128)(4,1)S(1)} %compare_reduce_fusion.4, ...), kind=kLoop, calls=%fused_computation.144 | loop fusion | flops 37888 | bytes 33904 | tf_op jit(solution)/shard_map/eq | solution.py:43
  155.9 3.6 %fusion.16 = bf16[8,1024,128]{2,1,0:T(8,128)(2,1)} fusion(bf16[1024,8,128]{2,0,1:T(8,128)(2,1)} %copy.76, pred[8,128]{1,0:T(8,128)(4,1)S(1)} %fusion.49, pred[1024]{0:T(1024)(128)(4,1)S(1)} %fusion.46), kind=kLoop, calls=%fused_computation.35 | loop fusion | flops 2097152 | bytes 4196352 | tf_op jit(solution)/shard_map/jit(_where)/select_n | solution.py:113
  161.1 5.7 %scatter_fusion = bf16[1024,8,128]{2,0,1:T(8,128)(2,1)} fusion(bf16[1024,8,128]{2,0,1:T(8,128)(2,1)} %broadcast_in_dim.16.clone, s32[8]{0:T(128)S(1)} %fusion.61, bf16[8,1024,128]{2,1,0:T(8,128)(2,1)} %fusion.16), kind=kCustom, calls=%fused_computation.1 | custom fusion | bytes 6291488 | tf_op jit(solution)/shard_map/scatter | solution.py:119
  166.8 53.7 %all_to_all.10 = bf16[1024,8,128]{2,0,1:T(8,128)(2,1)S(1)} all-to-all(bf16[1024,8,128]{2,0,1:T(8,128)(2,1)} %scatter_fusion), channel_id=1, replica_groups=mesh['sky'=8,'band'=4] {'sky'}, dimensions={1} | all-to-all | bytes 4194304 | tf_op jit(solution)/shard_map/all_to_all | solution.py:125
  226.9 3.3 %collective-permute-start.1 = (bf16[1024,15]{1,0:T(8,128)(2,1)S(1)}, bf16[1024,15]{1,0:T(8,128)(2,1)S(1)}, u32[]{:S(2)}, u32[]{:S(2)}) collective-permute-start(bf16[1024,15]{1,0:T(8,128)(2,1)S(1)} %get-tuple-element.11), channel_id=1, source_target_pairs={{4,0},{8,4},{12,8},{16,12},{20,16},{24,20},{28,24},{0,28},{5,1},{9... | collective-permute-start | bytes 92168 | tf_op jit(solution)/shard_map/ppermute | solution.py:21
  230.7 9.0 %collective-permute-done = bf16[1024,15]{1,0:T(8,128)(2,1)S(1)} collective-permute-done((bf16[1024,15]{1,0:T(8,128)(2,1)S(1)}, bf16[1024,15]{1,0:T(8,128)(2,1)S(1)}, u32[]{:S(2)}, u32[]{:S(2)}) %collective-permute-start) | collective-permute-done | bytes 30752 | tf_op jit(solution)/shard_map/ppermute | solution.py:18
  243.6 3.2 %copy.81 = f32[1,1,1024,1024]{2,3,1,0:T(8,128)} copy(bf16[1,1,1024,1024]{3,2,1,0:T(8,128)(2,1)S(1)} %bitcast.247) | data formatting | bytes 6291456 | tf_op jit(solution)/shard_map/convert_element_type | solution.py:90
  247.6 29.6 %all-gather.2.cloned.1.call-done = bf16[1024,1024]{1,0:T(8,128)(2,1)} async-done(((bf16[1024,128]{1,0:T(8,128)(2,1)}), bf16[1024,1024]{1,0:T(8,128)(2,1)}) %all-gather.2.cloned.1.call-update) | async-done | bytes 2097168 | tf_op jit(solution)/shard_map/all_gather | solution.py:86
  277.1 3.9 %copy.78 = bf16[1024,1024]{0,1:T(8,128)(2,1)} copy(bf16[1024,1024]{1,0:T(8,128)(2,1)} %all-gather.2.cloned.1.call-done) | data formatting | bytes 4194304 | tf_op jit(solution)/shard_map/all_gather | solution.py:86
  281.1 3.0 copy.79
  289.1 4.1 %subtract_convert_fusion = bf16[1,1,1024,1024]{2,3,1,0:T(8,128)(2,1)} fusion(f32[1,1,1024,1024]{2,3,1,0:T(8,128)} %copy.81, bf16[1,1,1024,1024]{2,3,1,0:T(8,128)(2,1)S(1)} %bitcast.249, pred[1024]{0:T(1024)(128)(4,1)S(1)} %broadcast_bitcast_fusion), kind=kLoop, calls=%fused_computation.10 | loop fusion | flops 4194304 | bytes 8389632 | tf_op jit(solution)/shard_map/convert_element_type | solution.py:90
  293.2 3.9 %copy.82 = bf16[1,1,1024,1024]{3,2,1,0:T(8,128)(2,1)} copy(bf16[1,1,1024,1024]{2,3,1,0:T(8,128)(2,1)} %subtract_convert_fusion) | data formatting | bytes 4194304
  (98 shorter events, 48.8 us)
Async XLA Ops:
  11.1 0.7 copy-start.3
  11.1 0.7 copy-start.4
  46.3 8.2 %copy-start = (bf16[9,1024,1024]{2,1,0:T(8,128)(2,1)S(1)}, bf16[9,1024,1024]{2,1,0:T(8,128)(2,1)}, u32[]{:S(2)}) copy-start(bf16[9,1024,1024]{2,1,0:T(8,128)(2,1)} %copy.67) | copy-start | bytes 56623108
  69.2 2.4 copy-start.5
  92.4 74.4 %all-to-all-start.1 = ((bf16[1024,8,128]{2,0,1:T(8,128)(2,1)}), bf16[1024,8,128]{2,0,1:T(8,128)(2,1)}, u32[]{:S(2)}, u32[]{:S(2)}) async-start(bf16[1024,8,128]{2,0,1:T(8,128)(2,1)} %scatter_fusion.1), calls=%async_computation.1 | async-start | bytes 4194304 | tf_op jit(solution)/shard_map/all_to_all | solution.py:124
  99.8 177.4 %all-gather.2.cloned.1.call-start = ((), (), s32[]{:S(2)}) async-start(), calls=%async_computation.3 | async-start | bytes 2359296 | tf_op jit(solution)/shard_map/all_gather | solution.py:86
  103.7 5.1 %copy-start.2 = (s32[1,1,2,35]{3,2,1,0:T(2,128)S(1)}, s32[1,1,2,35]{3,2,1,0:T(2,128)}, u32[]{:S(2)}) copy-start(s32[1,1,2,35]{3,2,1,0:T(2,128)} %param.10) | copy-start | bytes 844
  222.9 7.2 %copy-start.6 = (f32[1,31]{1,0:T(1,128)S(1)}, f32[1,31]{1,0:T(1,128)}, u32[]{:S(2)}) copy-start(f32[1,31]{1,0:T(1,128)} %param.15) | copy-start | bytes 376
  223.7 18.1 %copy-start.1 = (bf16[1024,128]{1,0:T(8,128)(2,1)S(1)}, bf16[1024,128]{1,0:T(8,128)(2,1)}, u32[]{:S(2)}) copy-start(bf16[1024,128]{1,0:T(8,128)(2,1)} %divide_convert_fusion) | copy-start | bytes 786436
  223.8 73.3 %reduce-scatter.2.cloned.1.call-start = ((), (), s32[]{:S(2)}) async-start(), calls=%async_computation.4 | async-start | bytes 655360 | tf_op jit(solution)/shard_map/reduce_scatter | solution.py:148
  225.3 14.3 %collective-permute-start = (bf16[1024,15]{1,0:T(8,128)(2,1)S(1)}, bf16[1024,15]{1,0:T(8,128)(2,1)S(1)}, u32[]{:S(2)}, u32[]{:S(2)}) collective-permute-start(bf16[1024,15]{1,0:T(8,128)(2,1)S(1)} %get-tuple-element.10), channel_id=1, source_target_pairs={{0,4},{4,8},{8,12},{12,16},{16,20},{20,24},{24,28},{28,0},{1,5},{5... | collective-permute-start | bytes 92168 | tf_op jit(solution)/shard_map/ppermute | solution.py:18
  226.9 15.0 %collective-permute-start.1 = (bf16[1024,15]{1,0:T(8,128)(2,1)S(1)}, bf16[1024,15]{1,0:T(8,128)(2,1)S(1)}, u32[]{:S(2)}, u32[]{:S(2)}) collective-permute-start(bf16[1024,15]{1,0:T(8,128)(2,1)S(1)} %get-tuple-element.11), channel_id=1, source_target_pairs={{4,0},{8,4},{12,8},{16,12},{20,16},{24,20},{28,24},{0,28},{5,1},{9... | collective-permute-start | bytes 92168 | tf_op jit(solution)/shard_map/ppermute | solution.py:21
Sparse Core Ops, SparseCore 0:
  223.9 53.1 all-gather.1
Sparse Core Ops, SparseCore 1:
  243.6 20.2 reduce-scatter.1
where the time goes:
time: 307 us; the launch traced here: 305 us
  local copies, waits for them, and re-layouts  102 us (33%)
  other arithmetic  57.9 us (19%)
  blocking collectives  53.7 us (17%)
  waiting for transfers between devices  40.8 us (13%)
  matrix products  22.3 us (7%)
  between operations  15.7 us (5%)
  starting transfers between devices  12.2 us (4%)
    all_to_all x1, blocking collectives, body(): lax.all_to_all(send_weight, 'sky', split_axis=1, concat_axis=1, tiled=True)  53.7 us
    unnamed x39, local copies, waits for them, and re-layouts  35.3 us
    eq x2, other arithmetic, keep_pixels(): return jnp.logical_and(row_bits[:, None] == 0, column_bits[None, :] == 0)  35.2 us
    all_gather x1, waiting for transfers between devices, subtract_template(): lax.all_gather(template, 'sky', axis=1, tiled=True)  29.6 us
    convert_element_type x1, local copies, waits for them, and re-layouts, psf_match(): column_pass.reshape(NB, side_length, side_length).astype(jnp.bfloat16)  24.6 us
    scatter x2, local copies, waits for them, and re-layouts, body(): empty_slots.at[:, own_columns, :]  11.4 us
    dot_general x1, matrix products, psf_match(): jnp.einsum('ikwx,kwt->itx', row_blocks, row_band, preferred_element_type=...  9.89 us
    dot_general x1, matrix products, psf_match(): jnp.einsum('jyw,kwt->kyjt', blocks, column_band, preferred_element_type=j...  9.18 us
  transfers between devices with their start and end apart: 5, of which 3 were waited for; matrix products, arithmetic and copies ran while one was open for 31% of the time, Pallas kernels for 0%

commit v1 on v0

--- a/solution.py
+++ b/solution.py
@@ -83,9 +83,12 @@
 
 
 def subtract_template(template, matched, own_columns, side_length, sky_count):
-    gathered = lax.all_gather(template, "sky", axis=1, tiled=True).reshape(
-        side_length, sky_count, TILE
-    )
+
+    def carry_pools_on_mesh(where_dim, unit):
+        state_next = jax.lax.all_gather(unit, "sky")
+        return jnp.concatenate(state_next, axis=where_dim)
+
+    gathered = carry_pools_on_mesh(1, template).reshape(side_length, sky_count, TILE)
     picked = jnp.take(gathered, own_columns, axis=1).reshape(side_length, side_length)
     return (matched.astype(jnp.float32) - picked.astype(jnp.float32)).astype(jnp.bfloat16)
 

time: 307 us -> 300 us (0.977)
  local copies, waits for them, and re-layouts: 102 us -> 96.4 us
    all_gather x1 -> x0, local copies, waits for them, and re-layouts: 3.93 us -> none  [subtract_template(): lax.all_gather(template, 'sky', axis=1, tiled=True)]
  transfers between devices with their start and end apart: 5 -> 5, of which waited for: 3 -> 3; matrix products, arithmetic and copies ran while one was open for 31% -> 30% of each run, Pallas kernels for 0% -> 0%
where the time goes in v1:
time: 300 us; the launch traced here: 298 us
  local copies, waits for them, and re-layouts  96.4 us (32%)
  other arithmetic  57.9 us (19%)
  blocking collectives  53.7 us (18%)
  waiting for transfers between devices  39.5 us (13%)
  matrix products  22.3 us (7%)
  between operations  15.7 us (5%)
  starting transfers between devices  12.2 us (4%)
    all_to_all x1, blocking collectives, body(): lax.all_to_all(send_weight, 'sky', split_axis=1, concat_axis=1, tiled=True)  53.7 us
    unnamed x39, local copies, waits for them, and re-layouts  35.3 us
    eq x2, other arithmetic, keep_pixels(): return jnp.logical_and(row_bits[:, None] == 0, column_bits[None, :] == 0)  35.2 us
    all_gather x1, waiting for transfers between devices, carry_pools_on_mesh(): state_next = jax.lax.all_gather(unit, 'sky')  28.3 us
    convert_element_type x1, local copies, waits for them, and re-layouts, psf_match(): column_pass.reshape(NB, side_length, side_length).astype(jnp.bfloat16)  24.6 us
    scatter x2, local copies, waits for them, and re-layouts, body(): empty_slots.at[:, own_columns, :]  11.4 us
    dot_general x1, matrix products, psf_match(): jnp.einsum('ikwx,kwt->itx', row_blocks, row_band, preferred_element_type=...  9.89 us
    dot_general x1, matrix products, psf_match(): jnp.einsum('jyw,kwt->kyjt', blocks, column_band, preferred_element_type=j...  9.18 us
  transfers between devices with their start and end apart: 5, of which 3 were waited for; matrix products, arithmetic and copies ran while one was open for 30% of the time, Pallas kernels for 0%

profile of v1, /device:TPU:0, one launch (start us, length us, event | category | flops | bytes accessed | tf_op | source)
XLA Modules:
  0.0 297.7 jit_solution(8054220407176057670)
XLA Ops:
  8.0 2.9 copy.46
  12.4 9.2 %convolution_convert_fusion = bf16[9,128,8,1024]{3,1,2,0:T(8,128)(2,1)} fusion(bf16[8,1024,152]{1,2,0:T(8,128)(2,1)S(1)} %fusion.34, bf16[9,152,128,1]{2,0,1,3:T(8,128)(2,1)S(1)} %fusion.19), kind=kOutput, calls=%fused_computation.5 | convolution fusion | flops 2878341120 | bytes 21714944 | tf_op jit(solution)/shard_map/jyw,kwt->kyjt/dot_general | solution.py:60
  21.6 24.6 %copy.48 = bf16[9,1024,1024]{2,1,0:T(8,128)(2,1)} copy(bf16[9,1024,1024]{1,2,0:T(8,128)(2,1)} %bitcast.239) | data formatting | bytes 37748736 | tf_op jit(solution)/shard_map/convert_element_type | solution.py:63
  46.3 4.3 %fusion.2 = bf16[8,9,152,1024]{3,2,1,0:T(8,128)(2,1)} fusion(bf16[9,1024,1024]{2,1,0:T(8,128)(2,1)} %copy.48), kind=kLoop, calls=%fused_computation.13 | loop fusion | bytes 21676032
  50.6 3.8 %copy-done = bf16[9,1024,1024]{2,1,0:T(8,128)(2,1)S(1)} copy-done((bf16[9,1024,1024]{2,1,0:T(8,128)(2,1)S(1)}, bf16[9,1024,1024]{2,1,0:T(8,128)(2,1)}, u32[]{:S(2)}) %copy-start) | copy-done | bytes 18874392
  72.2 9.9 %bitcast_convert_fusion = bf16[128,8,1024]{2,0,1:T(8,128)(2,1)S(1)} fusion(bf16[8,9,152,1024]{3,2,1,0:T(8,128)(2,1)} %fusion.4, bf16[9,152,128]{2,0,1:T(8,128)(2,1)S(1)} %fusion.20), kind=kOutput, calls=%fused_computation.9 | convolution fusion | flops 2869952512 | bytes 24860672 | tf_op jit(solution)/shard_map/ikwx,kwt->itx/dot_general | solution.py:73
  86.7 5.7 %scatter_fusion.1 = bf16[1024,8,128]{2,0,1:T(8,128)(2,1)} fusion(bf16[1024,8,128]{2,0,1:T(8,128)(2,1)} %broadcast_in_dim.16.clone.1, s32[8]{0:T(128)S(1)} %fusion.61, bf16[8,1024,128]{2,1,0:T(8,128)(2,1)} %bitcast.250), kind=kCustom, calls=%fused_computation.2 | custom fusion | bytes 6291488 | tf_op jit(solution)/shard_map/scatter | solution.py:119
  92.4 7.3 %all-to-all-start.1 = ((bf16[1024,8,128]{2,0,1:T(8,128)(2,1)}), bf16[1024,8,128]{2,0,1:T(8,128)(2,1)}, u32[]{:S(2)}, u32[]{:S(2)}) async-start(bf16[1024,8,128]{2,0,1:T(8,128)(2,1)} %scatter_fusion.1), calls=%async_computation.1 | async-start | bytes 4194304 | tf_op jit(solution)/shard_map/all_to_all | solution.py:127
  99.8 3.9 %copy.56 = bf16[1,1,1024,1024]{2,3,1,0:T(8,128)(2,1)} copy(bf16[1,1,1024,1024]{3,2,1,0:T(8,128)(2,1)} %param.9) | data formatting | bytes 4194304 | tf_op args[1]
  103.7 3.9 %copy.57 = bf16[1024,8,128]{2,0,1:T(8,128)(2,1)} copy(bf16[1024,8,128]{0,2,1:T(8,128)(2,1)} %bitcast.254) | data formatting | bytes 4194304 | tf_op jit(solution)/shard_map/squeeze | solution.py:115
  110.2 4.6 %compare_select_fusion.2 = s32[1024,1]{0,1:T(1,128)S(1)} fusion(s32[]{:T(128)} %bitcast.99, s32[]{:T(128)} %bitcast.100, s32[]{:T(128)} %bitcast.101, s32[]{:T(128)} %bitcast.102, s32[]{:T(128)} %bitcast.103, s32[]{:T(128)} %bitcast.105, s32[]{:T(128)} %bitcast.104), kind=kLoop, calls=%fused_computation.125 | loop fusion | flops 23552 | bytes 4124 | tf_op jit(solution)/shard_map/gather | solution.py:41
  116.3 4.4 %compare_select_fusion.1 = s32[1024,1]{0,1:T(1,128)S(1)} fusion(s32[]{:T(128)} %bitcast.63, s32[]{:T(128)} %bitcast.64, s32[]{:T(128)} %bitcast.65, s32[]{:T(128)} %bitcast.66, s32[]{:T(128)} %bitcast.67, s32[]{:T(128)} %bitcast.69, s32[]{:T(128)} %bitcast.68), kind=kLoop, calls=%fused_computation.124 | loop fusion | flops 23552 | bytes 4124 | tf_op jit(solution)/shard_map/gather | solution.py:42
  120.6 17.6 %fusion.49 = pred[8,128]{1,0:T(8,128)(4,1)S(1)} fusion(pred[1024]{0:T(1024)(128)(4,1)S(1)} %compare_reduce_fusion, pred[1024]{0:T(1024)(128)(4,1)S(1)} %compare_reduce_fusion.1, pred[1024]{0:T(1024)(128)(4,1)S(1)} %compare_reduce_fusion.2, pred[1024]{0:T(1024)(128)(4,1)S(1)} %compare_reduce_fusion.3, pred[1024]{0:T(1024)(128)(4,1)S(1)} %compare_reduce_fusion.4, ...), kind=kLoop, calls=%fused_computation.147 | loop fusion | flops 39936 | bytes 33904 | tf_op jit(solution)/shard_map/eq | solution.py:43
  138.3 17.6 %fusion.46 = pred[1024]{0:T(1024)(128)(4,1)S(1)} fusion(pred[1024]{0:T(1024)(128)(4,1)S(1)} %compare_reduce_fusion, pred[1024]{0:T(1024)(128)(4,1)S(1)} %compare_reduce_fusion.1, pred[1024]{0:T(1024)(128)(4,1)S(1)} %compare_reduce_fusion.2, pred[1024]{0:T(1024)(128)(4,1)S(1)} %compare_reduce_fusion.3, pred[1024]{0:T(1024)(128)(4,1)S(1)} %compare_reduce_fusion.4, ...), kind=kLoop, calls=%fused_computation.144 | loop fusion | flops 37888 | bytes 33904 | tf_op jit(solution)/shard_map/eq | solution.py:43
  155.9 3.6 %fusion.16 = bf16[8,1024,128]{2,1,0:T(8,128)(2,1)} fusion(bf16[1024,8,128]{2,0,1:T(8,128)(2,1)} %copy.57, pred[8,128]{1,0:T(8,128)(4,1)S(1)} %fusion.49, pred[1024]{0:T(1024)(128)(4,1)S(1)} %fusion.46), kind=kLoop, calls=%fused_computation.35 | loop fusion | flops 2097152 | bytes 4196352 | tf_op jit(solution)/shard_map/jit(_where)/select_n | solution.py:116
  161.1 5.7 %scatter_fusion = bf16[1024,8,128]{2,0,1:T(8,128)(2,1)} fusion(bf16[1024,8,128]{2,0,1:T(8,128)(2,1)} %broadcast_in_dim.16.clone, s32[8]{0:T(128)S(1)} %fusion.61, bf16[8,1024,128]{2,1,0:T(8,128)(2,1)} %fusion.16), kind=kCustom, calls=%fused_computation.1 | custom fusion | bytes 6291488 | tf_op jit(solution)/shard_map/scatter | solution.py:122
  166.8 53.7 %all_to_all.10 = bf16[1024,8,128]{2,0,1:T(8,128)(2,1)S(1)} all-to-all(bf16[1024,8,128]{2,0,1:T(8,128)(2,1)} %scatter_fusion), channel_id=1, replica_groups=mesh['sky'=8,'band'=4] {'sky'}, dimensions={1} | all-to-all | bytes 4194304 | tf_op jit(solution)/shard_map/all_to_all | solution.py:128
  226.9 3.3 %collective-permute-start.1 = (bf16[1024,15]{1,0:T(8,128)(2,1)S(1)}, bf16[1024,15]{1,0:T(8,128)(2,1)S(1)}, u32[]{:S(2)}, u32[]{:S(2)}) collective-permute-start(bf16[1024,15]{1,0:T(8,128)(2,1)S(1)} %get-tuple-element.9), channel_id=1, source_target_pairs={{4,0},{8,4},{12,8},{16,12},{20,16},{24,20},{28,24},{0,28},{5,1},{9... | collective-permute-start | bytes 92168 | tf_op jit(solution)/shard_map/ppermute | solution.py:21
  230.7 9.0 %collective-permute-done = bf16[1024,15]{1,0:T(8,128)(2,1)S(1)} collective-permute-done((bf16[1024,15]{1,0:T(8,128)(2,1)S(1)}, bf16[1024,15]{1,0:T(8,128)(2,1)S(1)}, u32[]{:S(2)}, u32[]{:S(2)}) %collective-permute-start) | collective-permute-done | bytes 30752 | tf_op jit(solution)/shard_map/ppermute | solution.py:18
  243.6 3.0 %copy.60 = f32[1,1,1024,1024]{2,3,1,0:T(8,128)} copy(bf16[1,1,1024,1024]{3,2,1,0:T(8,128)(2,1)S(1)} %bitcast.249) | data formatting | bytes 6291456 | tf_op jit(solution)/shard_map/convert_element_type | solution.py:93
  247.4 28.3 %all-gather.3.cloned.1.call-done = bf16[8192,128]{1,0:T(8,128)(2,1)} async-done(((bf16[1024,128]{1,0:T(8,128)(2,1)}), bf16[8192,128]{1,0:T(8,128)(2,1)}) %all-gather.3.cloned.1.call-update) | async-done | bytes 2097168 | tf_op jit(solution)/shard_map/all_gather | solution.py:88
  275.6 3.7 %gather_fusion = bf16[8,1024,128]{2,1,0:T(8,128)(2,1)} fusion(bf16[1024,8,128]{2,0,1:T(8,128)(2,1)} %bitcast.256, s32[1024]{0:T(1024)S(1)} %pad_clamp_fusion), kind=kCustom, calls=%fused_computation | custom fusion | bytes 4194336 | tf_op jit(solution)/shard_map/jit(_take)/gather | solution.py:92
  282.2 4.1 %subtract_convert_fusion = bf16[1,1,1024,1024]{2,3,1,0:T(8,128)(2,1)} fusion(f32[1,1,1024,1024]{2,3,1,0:T(8,128)} %copy.60, bf16[1,1,1024,1024]{2,3,1,0:T(8,128)(2,1)S(1)} %bitcast.251, pred[1024]{0:T(1024)(128)(4,1)S(1)} %broadcast_bitcast_fusion), kind=kLoop, calls=%fused_computation.10 | loop fusion | flops 4194304 | bytes 8389632 | tf_op jit(solution)/shard_map/convert_element_type | solution.py:93
  286.3 3.9 %copy.61 = bf16[1,1,1024,1024]{3,2,1,0:T(8,128)(2,1)} copy(bf16[1,1,1024,1024]{2,3,1,0:T(8,128)(2,1)} %subtract_convert_fusion) | data formatting | bytes 4194304
  (96 shorter events, 43.8 us)
Async XLA Ops:
  11.1 0.7 copy-start.3
  11.1 0.7 copy-start.4
  46.3 8.2 %copy-start = (bf16[9,1024,1024]{2,1,0:T(8,128)(2,1)S(1)}, bf16[9,1024,1024]{2,1,0:T(8,128)(2,1)}, u32[]{:S(2)}) copy-start(bf16[9,1024,1024]{2,1,0:T(8,128)(2,1)} %copy.48) | copy-start | bytes 56623108
  69.2 2.4 copy-start.5
  92.4 74.4 %all-to-all-start.1 = ((bf16[1024,8,128]{2,0,1:T(8,128)(2,1)}), bf16[1024,8,128]{2,0,1:T(8,128)(2,1)}, u32[]{:S(2)}, u32[]{:S(2)}) async-start(bf16[1024,8,128]{2,0,1:T(8,128)(2,1)} %scatter_fusion.1), calls=%async_computation.1 | async-start | bytes 4194304 | tf_op jit(solution)/shard_map/all_to_all | solution.py:127
  99.8 175.9 %all-gather.3.cloned.1.call-start = ((), (), s32[]{:S(2)}) async-start(), calls=%async_computation.4 | async-start | bytes 2359296 | tf_op jit(solution)/shard_map/all_gather | solution.py:88
  103.7 5.1 %copy-start.2 = (s32[1,1,2,35]{3,2,1,0:T(2,128)S(1)}, s32[1,1,2,35]{3,2,1,0:T(2,128)}, u32[]{:S(2)}) copy-start(s32[1,1,2,35]{3,2,1,0:T(2,128)} %param.10) | copy-start | bytes 844
  222.9 7.2 %copy-start.6 = (f32[1,31]{1,0:T(1,128)S(1)}, f32[1,31]{1,0:T(1,128)}, u32[]{:S(2)}) copy-start(f32[1,31]{1,0:T(1,128)} %param.15) | copy-start | bytes 376
  223.7 18.1 %copy-start.1 = (bf16[1024,128]{1,0:T(8,128)(2,1)S(1)}, bf16[1024,128]{1,0:T(8,128)(2,1)}, u32[]{:S(2)}) copy-start(bf16[1024,128]{1,0:T(8,128)(2,1)} %divide_convert_fusion) | copy-start | bytes 786436
  223.8 66.4 %reduce-scatter.2.cloned.1.call-start = ((), (), s32[]{:S(2)}) async-start(), calls=%async_computation.3 | async-start | bytes 655360 | tf_op jit(solution)/shard_map/reduce_scatter | solution.py:151
  225.3 14.3 %collective-permute-start = (bf16[1024,15]{1,0:T(8,128)(2,1)S(1)}, bf16[1024,15]{1,0:T(8,128)(2,1)S(1)}, u32[]{:S(2)}, u32[]{:S(2)}) collective-permute-start(bf16[1024,15]{1,0:T(8,128)(2,1)S(1)} %get-tuple-element.8), channel_id=1, source_target_pairs={{0,4},{4,8},{8,12},{12,16},{16,20},{20,24},{24,28},{28,0},{1,5},{5... | collective-permute-start | bytes 92168 | tf_op jit(solution)/shard_map/ppermute | solution.py:18
  226.9 15.0 %collective-permute-start.1 = (bf16[1024,15]{1,0:T(8,128)(2,1)S(1)}, bf16[1024,15]{1,0:T(8,128)(2,1)S(1)}, u32[]{:S(2)}, u32[]{:S(2)}) collective-permute-start(bf16[1024,15]{1,0:T(8,128)(2,1)S(1)} %get-tuple-element.9), channel_id=1, source_target_pairs={{4,0},{8,4},{12,8},{16,12},{20,16},{24,20},{28,24},{0,28},{5,1},{9... | collective-permute-start | bytes 92168 | tf_op jit(solution)/shard_map/ppermute | solution.py:21
Sparse Core Ops, SparseCore 0:
  223.9 51.6 all-gather.2
Sparse Core Ops, SparseCore 1:
  243.6 20.2 reduce-scatter.1
